TPU v7x, 512 devices: a whole 4x4x16 slice. The times are simulated.
512 devices in a mesh: dp: 64 (over z, y), owner: 8 (over x, core).
Axes of the slice: x: 4, y: 4, z: 16, core: 2. Of those that a mesh axis runs over, the one named last changes fastest.
Arguments:
- query_out: bfloat16 [512, 16384], P('dp', 'owner'), may hold values from -6 to 6
- query_in: bfloat16 [512, 8192], P('dp'), may hold values from -6 to 6
- train_out: bfloat16 [512, 16384], P('dp', 'owner'), may hold values from -6 to 6
- train_in: bfloat16 [512, 8192], P('dp'), may hold values from -6 to 6
- basis_out: bfloat16 [96, 256, 256], P('owner'), may hold values from -1 to 1, as said below
- basis_in: bfloat16 [64, 128, 128], P('dp'), may hold values from -1 to 1, as said below
- eigvals: float32 [24576, 8192], P('owner', 'dp'), may hold values from 0.1 to 10
- owner_map: int32 [64], replicated, may hold values from 0 to 7, as said below
Outputs:
- scores: float32 [8, 32], replicated
Inputs may be any that keep to these rules, and one draw needn't show every extreme that they name: owner_map[b] is the owner of hidden block b. Blocks form ranges of 8 in order; a block of range r is owned by r or by r xor 1. Of two such partner owners one holds exactly 12 blocks and keeps 12 // 2 of its own range, the other holds 4 blocks and keeps 8 - 12 // 2 of its own range. `basis_out`: each [256, 256] block is an orthogonal matrix rounded to bfloat16; block o * 12 + s belongs to the s-th block, in block order, that owner o holds; blocks past an owner's count are not read. `basis_in`: each [128, 128] block is an orthogonal matrix rounded to bfloat16.
All inputs are finite; a program needn't handle non-finite values.
Results may differ from a plain program's by a relative error of at most 0.0067.
Values may be sent and summed in bfloat16 or wider, within the bound.
No kernel may reach another device: no remote copies, remote signals or barrier semaphores. Data moves between devices by JAX's collectives and lax.ppermute only.
A program may use at most 64 MiB of HBM per device.

v0:
```python
import math
import jax
import jax.numpy as jnp
from jax import lax
from jax.sharding import PartitionSpec as P

NQ = 8
ET = 16
DAMPING = 0.1


def from_partner(array, axis, stride):
    return lax.ppermute(array, axis, [(i, i ^ 1 << stride) for i in range(lax.axis_size(axis))])


def slot_tables(owner_map, owner_index, blocks_own, capacity):
    pair_count = 2 * blocks_own
    pair_base = owner_index // 2 * pair_count
    pair_owner = lax.dynamic_slice_in_dim(owner_map, pair_base, pair_count)
    owned_mask = (pair_owner == owner_index).astype(jnp.int32)
    slot_rank = jnp.cumsum(owned_mask) - 1
    slot_ids = jnp.arange(capacity, dtype=jnp.int32)
    pair_hot = (owned_mask[:, None] == 1) & (slot_rank[:, None] == slot_ids[None, :])
    own_start = owner_index % 2 * blocks_own
    other_start = blocks_own - own_start
    keep_hot = lax.dynamic_slice_in_dim(pair_hot, own_start, blocks_own, 0)
    other_hot = lax.dynamic_slice_in_dim(pair_hot, other_start, blocks_own, 0)
    send_ids = jnp.arange(capacity // 2, dtype=jnp.int32)
    from_other = lax.dynamic_slice_in_dim(owned_mask, other_start, blocks_own)
    other_rank = jnp.cumsum(from_other) - 1
    arrive_hot = (from_other[:, None] == 1) & (other_rank[:, None] == send_ids[None, :])
    arrive_slot = jnp.dot(arrive_hot.T.astype(jnp.float32), other_hot.astype(jnp.float32))
    to_other = 1 - lax.dynamic_slice_in_dim(owned_mask, own_start, blocks_own)
    depart_rank = jnp.cumsum(to_other) - 1
    depart_hot = (to_other[:, None] == 1) & (depart_rank[:, None] == send_ids[None, :])
    return (
        keep_hot.astype(jnp.bfloat16),
        depart_hot.astype(jnp.bfloat16),
        arrive_slot.astype(jnp.bfloat16),
    )


def departing(tokens, depart_hot, block_width):
    blocks = tokens.reshape(tokens.shape[0], -1, block_width)
    return jnp.einsum("rpk,ps->rsk", blocks, depart_hot, preferred_element_type=jnp.float32).astype(
        jnp.bfloat16
    )


def to_slots(tokens, arrived, keep_hot, arrive_slot, block_width):
    blocks = tokens.reshape(tokens.shape[0], -1, block_width)
    kept_part = jnp.einsum("rpk,pc->rck", blocks, keep_hot, preferred_element_type=jnp.float32)
    moved_part = jnp.einsum("rsk,sc->rck", arrived, arrive_slot, preferred_element_type=jnp.float32)
    return (kept_part + moved_part).astype(jnp.bfloat16)


def rotate_outputs(slotted, basis_out):
    return jnp.einsum(
        "rck,ckl->rcl", slotted, basis_out, preferred_element_type=jnp.float32
    ).astype(jnp.bfloat16)


def rotate_inputs(columns_local, basis_in):
    token_count = columns_local.shape[0]
    blocks = columns_local.reshape(token_count, basis_in.shape[0], basis_in.shape[1])
    turned = jnp.einsum("tnb,nbc->tnc", blocks, basis_in, preferred_element_type=jnp.float32)
    return turned.astype(jnp.bfloat16).reshape(token_count, -1)


def condition(query_rot, query_act, eigvals, basis_in, basis_out):
    capacity, block_width = (basis_out.shape[0], basis_out.shape[1])
    in_blocks, in_width = (basis_in.shape[0], basis_in.shape[1])
    per_query = query_rot.shape[0] // NQ
    query_flat = query_rot.reshape(query_rot.shape[0], capacity * block_width)
    shifted = eigvals + DAMPING
    results = []
    for query_index in range(NQ):
        left_side = query_flat[query_index * per_query : (query_index + 1) * per_query]
        right_side = query_act[query_index * per_query : (query_index + 1) * per_query]
        moment = lax.dot_general(
            left_side, right_side, (((0,), (0,)), ((), ())), preferred_element_type=jnp.float32
        )
        damped = (moment / shifted).astype(jnp.bfloat16)
        half_back = jnp.einsum(
            "fnb,ncb->fnc",
            damped.reshape(-1, in_blocks, in_width),
            basis_in,
            preferred_element_type=jnp.float32,
        ).astype(jnp.bfloat16)
        restored = jnp.einsum(
            "ckl,cld->ckd",
            basis_out,
            half_back.reshape(capacity, block_width, -1),
            preferred_element_type=jnp.float32,
        ).astype(jnp.bfloat16)
        results.append(restored.reshape(capacity * block_width, -1))
    return jnp.stack(results)


def score_tokens(precond, train_slots, train_inputs, example_count):
    projected = jnp.einsum("tf,qfd->qtd", train_slots, precond, preferred_element_type=jnp.float32)
    per_token = jnp.sum(projected * train_inputs.astype(jnp.float32)[None], axis=2)
    token_ids = jnp.arange(train_slots.shape[0], dtype=jnp.int32)
    example_hot = (
        token_ids[:, None] // ET == jnp.arange(example_count, dtype=jnp.int32)[None, :]
    ).astype(jnp.float32)
    return jnp.dot(per_token, example_hot, precision=lax.Precision.HIGHEST)


def local(query_out, query_in, train_out, train_in, basis_out, basis_in, eigvals, owner_map):
    owner_index = lax.axis_index("owner")
    capacity = basis_out.shape[0]
    block_width = basis_out.shape[1]
    blocks_own = query_out.shape[1] // block_width
    query_local = query_out.shape[0]
    keep_hot, depart_hot, arrive_slot = slot_tables(owner_map, owner_index, blocks_own, capacity)
    query_cols, train_cols = (
        lax.all_to_all(query_in, "dp", split_axis=1, concat_axis=0, tiled=True),
        lax.all_to_all(train_in, "dp", split_axis=1, concat_axis=0, tiled=True),
    )
    query_act = rotate_inputs(query_cols, basis_in)
    example_count = train_cols.shape[0] // ET
    local_tokens = jnp.concatenate([query_out, train_out], 0)
    leaving = departing(local_tokens, depart_hot, block_width)
    arrived = from_partner(leaving, "owner", 0)
    slotted = to_slots(local_tokens, arrived, keep_hot, arrive_slot, block_width)
    query_rot = rotate_outputs(slotted[:query_local], basis_out)
    train_local = slotted[query_local:]
    query_all = lax.all_gather(query_rot, "dp", axis=0, tiled=True)
    precond = condition(query_all, query_act, eigvals, basis_in, basis_out)
    piece_slots = lax.all_gather(train_local, "dp", axis=0, tiled=True)
    row_count = piece_slots.shape[0]
    partial_scores = score_tokens(
        precond, piece_slots.reshape(row_count, -1), train_cols, example_count
    )
    scores = lax.psum(partial_scores, ("dp", "owner"))
    per_query = query_act.shape[0] // NQ
    hidden_total = query_out.shape[1] * lax.axis_size("owner")
    score_scale = 1.0 / math.sqrt(per_query * ET * hidden_total * query_in.shape[1])
    return scores * score_scale


def solution(mesh):
    in_specs = (
        P("dp", "owner"),
        P("dp", None),
        P("dp", "owner"),
        P("dp", None),
        P("owner", None, None),
        P("dp", None, None),
        P("owner", "dp"),
        P(),
    )
    out_specs = P()
    return jax.shard_map(local, mesh=mesh, in_specs=in_specs, out_specs=out_specs, check_vma=False)
```

profile of v0, /device:TPU:1, one launch (start us, length us, event | category | flops | bytes accessed | tf_op | source)
XLA Modules:
  0.0 418.7 jit_solution(11607726487385089527)
XLA Ops:
  6.5 0.8 broadcast_compare_fusion.2
  7.7 0.8 pad_maximum_fusion
  8.7 8.7 %collective-permute-start = (bf16[16,6,256]{2,1,0:T(8,128)(2,1)S(1)}, bf16[16,6,256]{2,1,0:T(8,128)(2,1)S(1)}, u32[]{:S(2)}, u32[]{:S(2)}) collective-permute-start(bf16[16,6,256]{2,1,0:T(8,128)(2,1)S(1)} %fusion.20), channel_id=1, source_target_pairs={{0,1},{1,0},{2,3},{3,2},{4,5},{5,4},{6,7},{7,6},{8,9},{9,8},{10,11... | collective-permute-start | bytes 147464 | tf_op jit(solution)/shard_map/ppermute | solution.py:13
  18.3 0.5 fusion.19
  18.8 0.9 fusion.21
  19.8 28.1 %all_to_all.29 = bf16[8,64,128]{2,0,1:T(8,128)(2,1)S(1)} all-to-all(bf16[8,64,128]{2,0,1:T(8,128)(2,1)S(1)} %bitcast.263), channel_id=1, replica_groups=mesh['dp'=64,'owner'=8] {'dp'}, dimensions={1} | all-to-all | bytes 262144 | tf_op jit(solution)/shard_map/all_to_all | solution.py:119
  47.9 6.4 %all-to-all-start = ((bf16[8,64,128]{2,0,1:T(8,128)(2,1)}), bf16[8,64,128]{2,0,1:T(8,128)(2,1)S(1)}, u32[]{:S(2)}, u32[]{:S(2)}) async-start(bf16[8,64,128]{2,0,1:T(8,128)(2,1)} %bitcast.12), calls=%async_computation | async-start | bytes 262144 | tf_op jit(solution)/shard_map/all_to_all | solution.py:118
  54.6 0.6 copy.120
  55.3 0.8 copy.123
  56.1 12.7 %all-to-all-done = bf16[8,64,128]{2,0,1:T(8,128)(2,1)S(1)} async-done(((bf16[8,64,128]{2,0,1:T(8,128)(2,1)}), bf16[8,64,128]{2,0,1:T(8,128)(2,1)S(1)}, u32[]{:S(2)}, u32[]{:S(2)}) %all-to-all-start) | async-done | bytes 131104 | tf_op jit(solution)/shard_map/all_to_all | solution.py:118
  68.8 0.9 fusion.18
  69.7 80.6 %all-gather.3.cloned.1.call-done = bf16[512,12,256]{2,0,1:T(8,128)(2,1)} async-done(((bf16[8,12,256]{2,0,1:T(8,128)(2,1)}), bf16[512,12,256]{2,0,1:T(8,128)(2,1)}) %all-gather.3.cloned.1.call-update) | async-done | bytes 3145744 | tf_op jit(solution)/shard_map/all_gather | solution.py:129
  150.3 3.3 slice_bitcast_fusion
  153.6 2.1 convolution_convert_fusion.7
  155.8 0.6 fusion.9
  156.4 0.4 copy.90
  157.1 1.0 copy.135
  158.1 3.1 convolution_convert_fusion.6
  161.2 1.8 fusion.10
  163.0 1.2 copy.93
  164.1 1.4 copy.113
  165.6 1.8 copy.136
  167.3 3.2 convolution_convert_fusion.5
  170.5 2.7 fusion.11
  173.2 2.3 copy.96
  175.5 2.3 copy.114
  177.7 1.8 copy.137
  179.6 3.2 convolution_convert_fusion.4
  182.8 2.7 fusion.12
  185.4 2.3 copy.99
  187.7 2.3 copy.115
  190.1 1.8 copy.138
  191.8 3.2 convolution_convert_fusion.3
  195.0 2.7 fusion.13
  197.7 2.3 copy.102
  200.0 2.3 copy.116
  202.3 1.8 copy.139
  204.1 3.2 convolution_convert_fusion.2
  207.3 2.7 fusion.14
  210.0 2.3 copy.105
  212.3 2.3 copy.117
  214.6 1.8 copy.140
  216.4 3.2 convolution_convert_fusion.1
  219.5 2.9 fusion.15
  222.4 2.3 copy.108
  224.7 2.4 copy.118
  227.1 0.8 copy.141
  227.9 3.2 convolution_convert_fusion
  231.1 2.7 fusion.16
  233.8 2.3 copy.111
  236.1 2.3 copy.119
  238.3 0.9 constant_dynamic-update-slice_fusion.7
  239.3 0.9 constant_dynamic-update-slice_fusion.6
  240.2 0.9 constant_dynamic-update-slice_fusion.5
  241.2 0.9 constant_dynamic-update-slice_fusion.4
  242.1 0.9 constant_dynamic-update-slice_fusion.3
  243.1 0.9 constant_dynamic-update-slice_fusion.2
  244.0 1.0 constant_dynamic-update-slice_fusion.1
  245.0 0.9 constant_dynamic-update-slice_fusion
  245.9 42.4 %all-gather.5.cloned.1.call-done = bf16[512,12,256]{2,0,1:T(8,128)(2,1)} async-done(((bf16[8,12,256]{2,0,1:T(8,128)(2,1)}), bf16[512,12,256]{2,0,1:T(8,128)(2,1)}) %all-gather.5.cloned.1.call-update) | async-done | bytes 3145744 | tf_op jit(solution)/shard_map/all_gather | solution.py:131
  288.4 4.7 %copy.121 = bf16[512,12,256]{0,2,1:T(8,128)(2,1)} copy(bf16[512,12,256]{2,0,1:T(8,128)(2,1)} %all-gather.5.cloned.1.call-done) | data formatting | bytes 6291456 | tf_op jit(solution)/shard_map/all_gather | solution.py:131
  293.1 7.1 %fusion.8 = f32[8,512]{1,0:T(8,128)S(1)} fusion(bf16[8,3072,128]{1,2,0:T(8,128)(2,1)} %constant_dynamic-update-slice_fusion, bf16[512,3072,1]{0,1,2:T(8,128)(2,1)} %bitcast.235, f32[512,128]{0,1:T(8,128)S(1)} %copy-done.7), kind=kOutput, calls=%fused_computation.25 | convolution fusion | flops 3222269952 | bytes 9715712 | tf_op jit(solution)/shard_map/tf,qfd->qtd/dot_general | solution.py:101
  300.5 110.8 %psum.7 = f32[8,32]{1,0:T(8,128)S(1)} all-reduce(f32[8,32]{1,0:T(8,128)S(1)} %fusion.39), channel_id=1, replica_groups=mesh['dp'=64,'owner'=8] {'dp','owner'}, use_global_device_ids=true, to_apply=%region_4.5 | all-reduce | flops 256 | bytes 2048 | tf_op jit(solution)/shard_map/psum | solution.py:136
  411.2 0.6 broadcast_multiply_fusion
  (44 shorter events, 2.3 us)
Async XLA Ops:
  6.5 12.3 %copy-start = (bf16[12,256,256]{2,1,0:T(8,128)(2,1)S(1)}, bf16[12,256,256]{2,1,0:T(8,128)(2,1)}, u32[]{:S(2)}) copy-start(bf16[12,256,256]{2,1,0:T(8,128)(2,1)} %param.12) | copy-start | bytes 4718596
  6.5 143.8 %all-gather.3.cloned.1.call-start = ((), (), s32[]{:S(2)}) async-start(), calls=%async_computation.2 | async-start | bytes 3194880 | tf_op jit(solution)/shard_map/all_gather | solution.py:129
  8.5 11.3 %copy-start.8 = (bf16[8,8192]{1,0:T(8,128)(2,1)S(1)}, bf16[8,8192]{1,0:T(8,128)(2,1)}, u32[]{:S(2)}) copy-start(bf16[8,8192]{1,0:T(8,128)(2,1)} %param.11) | copy-start | bytes 393220
  8.7 9.6 %collective-permute-start = (bf16[16,6,256]{2,1,0:T(8,128)(2,1)S(1)}, bf16[16,6,256]{2,1,0:T(8,128)(2,1)S(1)}, u32[]{:S(2)}, u32[]{:S(2)}) collective-permute-start(bf16[16,6,256]{2,1,0:T(8,128)(2,1)S(1)} %fusion.20), channel_id=1, source_target_pairs={{0,1},{1,0},{2,3},{3,2},{4,5},{5,4},{6,7},{7,6},{8,9},{9,8},{10,11... | collective-permute-start | bytes 147464 | tf_op jit(solution)/shard_map/ppermute | solution.py:13
  18.8 50.0 %copy-start.9 = (bf16[1,128,128]{2,1,0:T(8,128)(2,1)S(1)}, bf16[1,128,128]{2,1,0:T(8,128)(2,1)}, u32[]{:S(2)}) copy-start(bf16[1,128,128]{2,1,0:T(8,128)(2,1)} %param.13) | copy-start | bytes 98308
  47.9 20.9 %all-to-all-start = ((bf16[8,64,128]{2,0,1:T(8,128)(2,1)}), bf16[8,64,128]{2,0,1:T(8,128)(2,1)S(1)}, u32[]{:S(2)}, u32[]{:S(2)}) async-start(bf16[8,64,128]{2,0,1:T(8,128)(2,1)} %bitcast.12), calls=%async_computation | async-start | bytes 262144 | tf_op jit(solution)/shard_map/all_to_all | solution.py:118
  54.3 234.0 %all-gather.5.cloned.1.call-start = ((), (), s32[]{:S(2)}) async-start(), calls=%async_computation.3 | async-start | bytes 3194880 | tf_op jit(solution)/shard_map/all_gather | solution.py:131
  238.3 1.9 copy-start.1
  239.3 1.9 copy-start.2
  240.2 1.9 copy-start.3
  241.2 1.9 copy-start.4
  242.1 1.9 copy-start.5
  243.1 1.9 copy-start.6
  245.9 47.1 %copy-start.7 = (f32[512,128]{0,1:T(8,128)S(1)}, f32[512,128]{0,1:T(8,128)}, u32[]{:S(2)}) copy-start(f32[512,128]{0,1:T(8,128)} %copy.123) | copy-start | bytes 786436
Sparse Core Ops, SparseCore 0:
  19.9 130.3 all-gather.2
  153.2 135.1 all-gather.4
where the time goes:
time: 420 us; the launch traced here: 419 us
  blocking collectives  139 us (33%)
  waiting for transfers between devices  136 us (32%)
  local copies, waits for them, and re-layouts  58.8 us (14%)
  matrix products  53 us (13%)
  starting transfers between devices  15.4 us (4%)
  between operations  13.6 us (3%)
    psum x1, blocking collectives, local(): scores = lax.psum(partial_scores, ('dp', 'owner'))  111 us
    all_gather x1, waiting for transfers between devices, local(): query_all = lax.all_gather(query_rot, 'dp', axis=0, tiled=True)  80.6 us
    all_gather x1, waiting for transfers between devices, local(): piece_slots = lax.all_gather(train_local, 'dp', axis=0, tiled=True)  42.4 us
    all_to_all x1, blocking collectives, local(): lax.all_to_all(train_in, 'dp', split_axis=1, concat_axis=0, tiled=True)  28.1 us
    dot_general x8, matrix products, condition(): jnp.einsum('fnb,ncb->fnc', damped.reshape(-1, in_blocks, in_width), basis...  24.3 us
    dot_general x8, matrix products, condition(): jnp.einsum('ckl,cld->ckd', basis_out, half_back.reshape(capacity, block_w...  18.7 us
    another operation x9, local copies, waits for them, and re-layouts, condition(): return jnp.stack(results)  16.5 us
    convert_element_type x8, local copies, waits for them, and re-layouts, condition(): restored = jnp.einsum('ckl,cld->ckd', basis_out, half_back.reshape(capaci...  15.3 us
  transfers between devices with their start and end apart: 4, of which 4 were waited for; matrix products, arithmetic and copies ran while one was open for 24% of the time, Pallas kernels for 0%

commit v1 on v0

--- a/solution.py
+++ b/solution.py
@@ -133,7 +133,8 @@
     partial_scores = score_tokens(
         precond, piece_slots.reshape(row_count, -1), train_cols, example_count
     )
-    scores = lax.psum(partial_scores, ("dp", "owner"))
+    inner = lax.psum(partial_scores, "dp")
+    scores = lax.psum(inner, "owner")
     per_query = query_act.shape[0] // NQ
     hidden_total = query_out.shape[1] * lax.axis_size("owner")
     score_scale = 1.0 / math.sqrt(per_query * ET * hidden_total * query_in.shape[1])

time: 420 us -> 473 us (1.13)
  blocking collectives: 139 us -> 192 us
    psum x1 -> x2, blocking collectives: 111 us -> 163 us  [the longest x1 113 us: local(): inner = lax.psum(partial_scores, 'dp')]
  transfers between devices with their start and end apart: 4 -> 4, of which waited for: 4 -> 4; matrix products, arithmetic and copies ran while one was open for 24% -> 21% of each run, Pallas kernels for 0% -> 0%
where the time goes in v1:
time: 473 us; the launch traced here: 471 us
  blocking collectives  192 us (41%)
  waiting for transfers between devices  136 us (29%)
  local copies, waits for them, and re-layouts  58.6 us (12%)
  matrix products  53 us (11%)
  starting transfers between devices  15.4 us (3%)
  between operations  13.6 us (3%)
    psum x1, blocking collectives, local(): inner = lax.psum(partial_scores, 'dp')  113 us
    all_gather x1, waiting for transfers between devices, local(): query_all = lax.all_gather(query_rot, 'dp', axis=0, tiled=True)  80.6 us
    psum x1, blocking collectives, local(): scores = lax.psum(inner, 'owner')  50.5 us
    all_gather x1, waiting for transfers between devices, local(): piece_slots = lax.all_gather(train_local, 'dp', axis=0, tiled=True)  42.7 us
    all_to_all x1, blocking collectives, local(): lax.all_to_all(train_in, 'dp', split_axis=1, concat_axis=0, tiled=True)  28.1 us
    dot_general x8, matrix products, condition(): jnp.einsum('fnb,ncb->fnc', damped.reshape(-1, in_blocks, in_width), basis...  24.3 us
    dot_general x8, matrix products, condition(): jnp.einsum('ckl,cld->ckd', basis_out, half_back.reshape(capacity, block_w...  18.7 us
    another operation x9, local copies, waits for them, and re-layouts, condition(): return jnp.stack(results)  16.4 us
  transfers between devices with their start and end apart: 4, of which 4 were waited for; matrix products, arithmetic and copies ran while one was open for 21% of the time, Pallas kernels for 0%

profile of v1, /device:TPU:1, one launch (start us, length us, event | category | flops | bytes accessed | tf_op | source)
XLA Modules:
  0.0 471.4 jit_solution(7601752063701406957)
XLA Ops:
  6.5 0.8 broadcast_compare_fusion.2
  7.7 0.8 pad_maximum_fusion
  8.7 8.7 %collective-permute-start = (bf16[16,6,256]{2,1,0:T(8,128)(2,1)S(1)}, bf16[16,6,256]{2,1,0:T(8,128)(2,1)S(1)}, u32[]{:S(2)}, u32[]{:S(2)}) collective-permute-start(bf16[16,6,256]{2,1,0:T(8,128)(2,1)S(1)} %fusion.20), channel_id=1, source_target_pairs={{0,1},{1,0},{2,3},{3,2},{4,5},{5,4},{6,7},{7,6},{8,9},{9,8},{10,11... | collective-permute-start | bytes 147464 | tf_op jit(solution)/shard_map/ppermute | solution.py:13
  18.3 0.5 fusion.19
  18.8 0.9 fusion.21
  19.8 28.1 %all_to_all.29 = bf16[8,64,128]{2,0,1:T(8,128)(2,1)S(1)} all-to-all(bf16[8,64,128]{2,0,1:T(8,128)(2,1)S(1)} %bitcast.263), channel_id=1, replica_groups=mesh['dp'=64,'owner'=8] {'dp'}, dimensions={1} | all-to-all | bytes 262144 | tf_op jit(solution)/shard_map/all_to_all | solution.py:119
  47.9 6.4 %all-to-all-start = ((bf16[8,64,128]{2,0,1:T(8,128)(2,1)}), bf16[8,64,128]{2,0,1:T(8,128)(2,1)S(1)}, u32[]{:S(2)}, u32[]{:S(2)}) async-start(bf16[8,64,128]{2,0,1:T(8,128)(2,1)} %bitcast.12), calls=%async_computation | async-start | bytes 262144 | tf_op jit(solution)/shard_map/all_to_all | solution.py:118
  54.6 0.6 copy.120
  55.3 0.8 copy.123
  56.1 12.7 %all-to-all-done = bf16[8,64,128]{2,0,1:T(8,128)(2,1)S(1)} async-done(((bf16[8,64,128]{2,0,1:T(8,128)(2,1)}), bf16[8,64,128]{2,0,1:T(8,128)(2,1)S(1)}, u32[]{:S(2)}, u32[]{:S(2)}) %all-to-all-start) | async-done | bytes 131104 | tf_op jit(solution)/shard_map/all_to_all | solution.py:118
  68.8 0.9 fusion.18
  69.7 80.6 %all-gather.3.cloned.1.call-done = bf16[512,12,256]{2,0,1:T(8,128)(2,1)} async-done(((bf16[8,12,256]{2,0,1:T(8,128)(2,1)}), bf16[512,12,256]{2,0,1:T(8,128)(2,1)}) %all-gather.3.cloned.1.call-update) | async-done | bytes 3145744 | tf_op jit(solution)/shard_map/all_gather | solution.py:129
  150.3 3.3 slice_bitcast_fusion
  153.7 2.1 convolution_convert_fusion.7
  155.8 0.6 fusion.9
  157.1 1.0 copy.135
  158.1 3.1 convolution_convert_fusion.6
  161.2 1.8 fusion.10
  163.0 1.2 copy.93
  164.1 1.4 copy.113
  165.6 1.8 copy.136
  167.3 3.2 convolution_convert_fusion.5
  170.5 2.7 fusion.11
  173.2 2.3 copy.96
  175.5 2.3 copy.114
  177.7 1.8 copy.137
  179.5 3.2 convolution_convert_fusion.4
  182.7 2.7 fusion.12
  185.4 2.3 copy.99
  187.7 2.3 copy.115
  190.0 1.8 copy.138
  191.8 3.2 convolution_convert_fusion.3
  195.0 2.7 fusion.13
  197.6 2.3 copy.102
  199.9 2.3 copy.116
  202.2 1.8 copy.139
  204.0 3.2 convolution_convert_fusion.2
  207.2 2.7 fusion.14
  209.9 2.3 copy.105
  212.2 2.3 copy.117
  214.5 1.8 copy.140
  216.2 3.2 convolution_convert_fusion.1
  219.4 2.9 fusion.15
  222.3 2.3 copy.108
  224.6 2.3 copy.118
  226.9 0.8 copy.141
  227.7 3.2 convolution_convert_fusion
  230.9 2.7 fusion.16
  233.6 2.3 copy.111
  235.8 2.3 copy.119
  238.1 0.9 constant_dynamic-update-slice_fusion.7
  239.1 0.9 constant_dynamic-update-slice_fusion.6
  240.0 1.0 constant_dynamic-update-slice_fusion.5
  241.0 0.9 constant_dynamic-update-slice_fusion.4
  241.9 0.9 constant_dynamic-update-slice_fusion.3
  242.9 0.9 constant_dynamic-update-slice_fusion.2
  243.8 0.9 constant_dynamic-update-slice_fusion.1
  244.8 0.9 constant_dynamic-update-slice_fusion
  245.7 42.7 %all-gather.5.cloned.1.call-done = bf16[512,12,256]{2,0,1:T(8,128)(2,1)} async-done(((bf16[8,12,256]{2,0,1:T(8,128)(2,1)}), bf16[512,12,256]{2,0,1:T(8,128)(2,1)}) %all-gather.5.cloned.1.call-update) | async-done | bytes 3145744 | tf_op jit(solution)/shard_map/all_gather | solution.py:131
  288.4 4.7 copy.121
  293.1 7.1 %fusion.8 = f32[8,512]{1,0:T(8,128)S(1)} fusion(bf16[8,3072,128]{1,2,0:T(8,128)(2,1)} %constant_dynamic-update-slice_fusion, bf16[512,3072,1]{0,1,2:T(8,128)(2,1)} %bitcast.235, f32[512,128]{0,1:T(8,128)S(1)} %copy-done.7), kind=kOutput, calls=%fused_computation.25 | convolution fusion | flops 3222269952 | bytes 9715712 | tf_op jit(solution)/shard_map/tf,qfd->qtd/dot_general | solution.py:101
  300.5 113.0 %psum.14 = f32[8,32]{1,0:T(8,128)S(1)} all-reduce(f32[8,32]{1,0:T(8,128)S(1)} %fusion.39), channel_id=1, replica_groups=mesh['dp'=64,'owner'=8] {'dp'}, use_global_device_ids=true, to_apply=%region_4.5 | all-reduce | flops 256 | bytes 2048 | tf_op jit(solution)/shard_map/psum | solution.py:136
  413.4 50.5 %psum.15 = f32[8,32]{1,0:T(8,128)S(1)} all-reduce(f32[8,32]{1,0:T(8,128)S(1)} %psum.14), channel_id=1, replica_groups=mesh['dp'=64,'owner'=8] {'owner'}, use_global_device_ids=true, to_apply=%region_5.6 | all-reduce | flops 256 | bytes 2048 | tf_op jit(solution)/shard_map/psum | solution.py:137
  463.9 0.6 broadcast_multiply_fusion
  (45 shorter events, 2.6 us)
Async XLA Ops:
  6.5 12.3 %copy-start = (bf16[12,256,256]{2,1,0:T(8,128)(2,1)S(1)}, bf16[12,256,256]{2,1,0:T(8,128)(2,1)}, u32[]{:S(2)}) copy-start(bf16[12,256,256]{2,1,0:T(8,128)(2,1)} %param.12) | copy-start | bytes 4718596
  6.5 143.8 %all-gather.3.cloned.1.call-start = ((), (), s32[]{:S(2)}) async-start(), calls=%async_computation.2 | async-start | bytes 3194880 | tf_op jit(solution)/shard_map/all_gather | solution.py:129
  8.5 11.3 %copy-start.8 = (bf16[8,8192]{1,0:T(8,128)(2,1)S(1)}, bf16[8,8192]{1,0:T(8,128)(2,1)}, u32[]{:S(2)}) copy-start(bf16[8,8192]{1,0:T(8,128)(2,1)} %param.11) | copy-start | bytes 393220
  8.7 9.6 %collective-permute-start = (bf16[16,6,256]{2,1,0:T(8,128)(2,1)S(1)}, bf16[16,6,256]{2,1,0:T(8,128)(2,1)S(1)}, u32[]{:S(2)}, u32[]{:S(2)}) collective-permute-start(bf16[16,6,256]{2,1,0:T(8,128)(2,1)S(1)} %fusion.20), channel_id=1, source_target_pairs={{0,1},{1,0},{2,3},{3,2},{4,5},{5,4},{6,7},{7,6},{8,9},{9,8},{10,11... | collective-permute-start | bytes 147464 | tf_op jit(solution)/shard_map/ppermute | solution.py:13
  18.8 50.0 %copy-start.9 = (bf16[1,128,128]{2,1,0:T(8,128)(2,1)S(1)}, bf16[1,128,128]{2,1,0:T(8,128)(2,1)}, u32[]{:S(2)}) copy-start(bf16[1,128,128]{2,1,0:T(8,128)(2,1)} %param.13) | copy-start | bytes 98308
  47.9 20.9 %all-to-all-start = ((bf16[8,64,128]{2,0,1:T(8,128)(2,1)}), bf16[8,64,128]{2,0,1:T(8,128)(2,1)S(1)}, u32[]{:S(2)}, u32[]{:S(2)}) async-start(bf16[8,64,128]{2,0,1:T(8,128)(2,1)} %bitcast.12), calls=%async_computation | async-start | bytes 262144 | tf_op jit(solution)/shard_map/all_to_all | solution.py:118
  54.3 234.0 %all-gather.5.cloned.1.call-start = ((), (), s32[]{:S(2)}) async-start(), calls=%async_computation.3 | async-start | bytes 3194880 | tf_op jit(solution)/shard_map/all_gather | solution.py:131
  238.1 1.9 copy-start.1
  239.1 1.9 copy-start.2
  240.0 1.9 copy-start.3
  241.0 1.9 copy-start.4
  241.9 1.9 copy-start.5
  242.9 1.9 copy-start.6
  245.7 47.3 %copy-start.7 = (f32[512,128]{0,1:T(8,128)S(1)}, f32[512,128]{0,1:T(8,128)}, u32[]{:S(2)}) copy-start(f32[512,128]{0,1:T(8,128)} %copy.123) | copy-start | bytes 786436
Sparse Core Ops, SparseCore 0:
  19.9 130.3 all-gather.2
  153.2 135.1 all-gather.4
